TPU v7x, 32 devices: a whole 2x2x4 slice. The times are simulated.
32 devices in a mesh: lat: 8 (over z, core), lon: 4 (over y, x).
Axes of the slice: x: 2, y: 2, z: 4, core: 2. Of those that a mesh axis runs over, the one named last changes fastest.
Arguments:
- predicted_state: float32 [1440, 13312], P('lon', 'lat'), may hold values from -24 to 24
- verified_state: float32 [1440, 13312], P('lon', 'lat'), may hold values from -20 to 20
- normal_state: float32 [1440, 13312], P('lon', 'lat'), may hold values from -3 to 3
Outputs:
- energy_curves: float32 [3, 52, 721], replicated
- rms_error: float32 [52], replicated
- anomaly_corr: float32 [52], replicated
All inputs are finite; a program needn't handle non-finite values.
Results may differ from a plain program's by a relative error of at most 0.00005.
Values sent between devices are 32-bit elements; how exact they have to be, the bound alone decides.
A program may use at most 64 MiB of HBM per device.

v0:
```python
import jax
import jax.numpy as jnp
from jax import lax
from jax.sharding import PartitionSpec as P

FIELDS = 52
epsilon = 1e-06


def latitude_weights(lat_index, parallel_number):
    return jnp.cos(jnp.pi * ((lat_index.astype(jnp.float32) + 0.5) / parallel_number - 0.5))


def dft_table(lon_rows, lon_total, wave_count):
    longitudes = jnp.arange(lon_rows, dtype=jnp.int32)
    waves = jnp.arange(wave_count, dtype=jnp.int32)
    phase = longitudes[:, None] * waves[None, :] % lon_total
    angle = 2.0 * jnp.pi / lon_total * phase.astype(jnp.float32)
    return jnp.concatenate([jnp.cos(angle), -jnp.sin(angle)], axis=1)


def transform_columns(stacked, table):
    return lax.dot_general(
        stacked,
        table,
        (((0,), (0,)), ((), ())),
        precision=lax.Precision.HIGHEST,
        preferred_element_type=jnp.float32,
    )


def row_powers(fore_coeffs, true_coeffs, wave_count):
    diff_coeffs = fore_coeffs - true_coeffs

    def square(coeffs):
        return (
            coeffs[:, :wave_count] * coeffs[:, :wave_count]
            + coeffs[:, wave_count:] * coeffs[:, wave_count:]
        )

    return jnp.stack([square(fore_coeffs), square(true_coeffs), square(diff_coeffs)], axis=1)


def local(predicted_state, verified_state, normal_state):
    quantity_labels = FIELDS
    meridian_lines, meridian_number = predicted_state.shape
    parallel_lines = meridian_number // quantity_labels
    parallel_number = parallel_lines * lax.axis_size("lat")
    lon_devices = lax.axis_size("lon")
    lon_total = meridian_lines * lon_devices
    wave_count = lon_total // 2 + 1
    row_share = meridian_number // lon_devices
    lat_first = lax.axis_index("lat") * parallel_lines
    weights = latitude_weights(
        lat_first + jnp.arange(parallel_lines, dtype=jnp.int32), parallel_number
    )
    weight_total = jnp.sum(
        latitude_weights(jnp.arange(parallel_number, dtype=jnp.int32), parallel_number)
    )
    predicted_block = predicted_state.reshape(meridian_lines, parallel_lines, quantity_labels)
    observed_block = verified_state.reshape(meridian_lines, parallel_lines, quantity_labels)
    normal_block = normal_state.reshape(meridian_lines, parallel_lines, quantity_labels)
    mismatch_parts = predicted_block - observed_block
    predicted_anomalies = predicted_block - normal_block
    observed_anomalies = observed_block - normal_block
    broad_layout = weights[None, :, None]
    skill_terms = jnp.stack(
        [
            jnp.sum(broad_layout * mismatch_parts * mismatch_parts, axis=(0, 1)),
            jnp.sum(broad_layout * predicted_anomalies * observed_anomalies, axis=(0, 1)),
            jnp.sum(broad_layout * predicted_anomalies * predicted_anomalies, axis=(0, 1)),
            jnp.sum(broad_layout * observed_anomalies * observed_anomalies, axis=(0, 1)),
        ]
    )
    predicted_meridians = predicted_block.transpose(0, 2, 1).reshape(
        meridian_lines, meridian_number
    )
    true_cols = observed_block.transpose(0, 2, 1).reshape(meridian_lines, meridian_number)
    full_table = dft_table(lon_total, lon_total, wave_count)
    fore_blocks = predicted_meridians.reshape(meridian_lines, lon_devices, row_share)
    true_blocks = true_cols.reshape(meridian_lines, lon_devices, row_share)
    fore_part = lax.all_to_all(fore_blocks, "lon", split_axis=1, concat_axis=0, tiled=True)[:, 0, :]
    true_part = lax.all_to_all(true_blocks, "lon", split_axis=1, concat_axis=0, tiled=True)[:, 0, :]
    items = fore_part.shape[1]
    stacked = jnp.concatenate([fore_part, true_part], axis=1)
    coeffs = transform_columns(stacked, full_table)
    powers = row_powers(coeffs[:items], coeffs[items:], wave_count)
    share_start = lax.axis_index("lon") * row_share
    global_cols = share_start + jnp.arange(row_share, dtype=jnp.int32)
    field_of = global_cols // parallel_lines
    row_weights = latitude_weights(lat_first + global_cols % parallel_lines, parallel_number)
    row_scale = row_weights / (lon_total * lon_total * weight_total)
    weighted = powers.reshape(row_share, 3 * wave_count) * row_scale[:, None]
    field_index = jnp.arange(quantity_labels, dtype=jnp.int32)
    window = min(quantity_labels, row_share // parallel_lines + 2)
    first_field = share_start // parallel_lines
    window_index = jnp.arange(window, dtype=jnp.int32)
    offset = field_of - first_field
    selector = (offset[None, :] == window_index[:, None]).astype(jnp.float32)
    band_sum = jnp.dot(
        selector, weighted, precision=lax.Precision.HIGHEST, preferred_element_type=jnp.float32
    )
    band_sum = lax.psum(band_sum, "lat")
    gathered = lax.all_gather(band_sum, "lon", axis=0, tiled=True)
    slot_index = jnp.arange(lon_devices * window, dtype=jnp.int32)
    slot_field = slot_index // window * row_share // parallel_lines + slot_index % window
    placer = (slot_field[None, :] == field_index[:, None]).astype(jnp.float32)
    summed = jnp.dot(
        placer, gathered, precision=lax.Precision.HIGHEST, preferred_element_type=jnp.float32
    )
    energy_curves = summed.reshape(quantity_labels, 3, wave_count).transpose(1, 0, 2)
    skill_means = lax.psum(skill_terms, ("lat", "lon")) / (lon_total * weight_total)
    rms_error = jnp.sqrt(skill_means[0])
    anomaly_corr = skill_means[1] / jnp.sqrt(
        (skill_means[2] + epsilon) * (skill_means[3] + epsilon)
    )
    return (energy_curves, rms_error, anomaly_corr)


def solution(mesh):
    in_specs = (P("lon", "lat"), P("lon", "lat"), P("lon", "lat"))
    out_specs = (P(), P(), P())
    return jax.shard_map(local, mesh=mesh, in_specs=in_specs, out_specs=out_specs, check_vma=False)
```

profile of v0, /device:TPU:8, one launch (start us, length us, event | category | flops | bytes accessed | tf_op | source)
XLA Modules:
  0.0 275.4 jit_solution(18060614692774121550)
XLA Ops:
  7.2 3.2 %copy.26 = f32[360,1664]{0,1:T(8,128)} copy(f32[360,1664]{1,0:T(8,128)} %param.4) | data formatting | bytes 4792320 | tf_op args[1]
  10.4 2.4 reshape.125
  12.8 1.9 copy.27
  14.8 4.8 %all-to-all-start.1 = ((f32[360,4,416]{0,2,1:T(8,128)}), f32[360,4,416]{0,2,1:T(8,128)}, u32[]{:S(2)}, u32[]{:S(2)}) async-start(f32[360,4,416]{0,2,1:T(8,128)} %bitcast.41), calls=%async_computation.1 | async-start | bytes 5111808 | tf_op jit(solution)/shard_map/all_to_all | solution.py:83
  19.6 2.2 copy.23
  21.7 2.4 reshape.124
  24.2 2.1 copy.24
  26.4 0.1 mul.171
  26.5 23.2 %all-to-all-done.1 = f32[360,4,416]{0,2,1:T(8,128)} async-done(((f32[360,4,416]{0,2,1:T(8,128)}), f32[360,4,416]{0,2,1:T(8,128)}, u32[]{:S(2)}, u32[]{:S(2)}) %all-to-all-start.1) | async-done | bytes 2396192 | tf_op jit(solution)/shard_map/all_to_all | solution.py:83
  49.7 3.6 %all-to-all-start = ((f32[360,4,416]{0,2,1:T(8,128)}), f32[360,4,416]{0,2,1:T(8,128)S(1)}, u32[]{:S(2)}, u32[]{:S(2)}) async-start(f32[360,4,416]{0,2,1:T(8,128)} %bitcast.39), calls=%async_computation | async-start | bytes 5111808 | tf_op jit(solution)/shard_map/all_to_all | solution.py:82
  53.4 4.3 %fusion.17 = (f32[1664]{0:T(1024)S(1)}, f32[1664]{0:T(1024)S(1)}, f32[1664]{0:T(1024)S(1)}, f32[1664]{0:T(1024)S(1)}) fusion(f32[360,1664]{1,0:T(8,128)} %param.3, f32[360,1664]{1,0:T(8,128)} %param.4, f32[1664]{0:T(1024)S(1)} %mul.171, f32[360,1664]{1,0:T(8,128)} %param.5), kind=kLoop, calls=%fused_computation.26 | loop fusion | flops 8379904 | bytes 7221760 | tf_op jit(solution)/shard_map/reduce_sum | solution.py:69
  58.1 0.7 cosine_reduce_fusion
  60.1 55.8 %psum.15 = f32[4,52]{1,0:T(4,128)S(1)} all-reduce(f32[4,52]{1,0:T(4,128)S(1)} %pad_maximum_fusion.1), channel_id=1, replica_groups=mesh['lat'=8,'lon'=4] {'lat','lon'}, use_global_device_ids=true, to_apply=%region_10.11 | all-reduce | flops 208 | bytes 1664 | tf_op jit(solution)/shard_map/psum | solution.py:112
  116.0 0.5 multiply_bitcast_fusion
  116.5 19.7 %sine_negate_fusion = (f32[1440,721]{1,0:T(8,128)}, f32[1440,721]{1,0:T(8,128)}) fusion(), kind=kLoop, calls=%fused_computation.12 | loop fusion | flops 10382400 | bytes 8305920 | tf_op jit(solution)/shard_map/neg | solution.py:19
  136.2 4.8 %copy.28 = f32[4,360,1,416]{1,0,3,2:T(4,128)} copy(f32[4,360,1,416]{1,3,0,2:T(8,128)} %bitcast.7) | data formatting | bytes 4792320 | tf_op jit(solution)/shard_map/all_to_all | solution.py:83
  141.1 4.0 %squeeze.5 = f32[1440,416]{0,1:T(8,128)} reshape(f32[4,360,1,416]{1,0,3,2:T(4,128)} %copy.28) | data formatting | bytes 4792320 | tf_op jit(solution)/shard_map/squeeze | solution.py:83
  145.1 3.1 %copy.25 = f32[4,360,1,416]{1,0,3,2:T(4,128)} copy(f32[4,360,1,416]{1,3,0,2:T(8,128)S(1)} %bitcast.40) | data formatting | bytes 4792320 | tf_op jit(solution)/shard_map/all_to_all | solution.py:82
  148.2 4.2 %squeeze.4 = f32[1440,416]{0,1:T(8,128)} reshape(f32[4,360,1,416]{1,0,3,2:T(4,128)} %copy.25) | data formatting | bytes 4792320 | tf_op jit(solution)/shard_map/squeeze | solution.py:82
  152.4 29.4 %fusion = f32[832,1442]{1,0:T(8,128)S(1)} fusion(f32[1440,721]{1,0:T(8,128)} %get-tuple-element.20, f32[1440,721]{1,0:T(8,128)} %get-tuple-element.21, f32[1440,416]{0,1:T(8,128)S(1)} %copy-done.1, f32[1440,416]{0,1:T(8,128)} %squeeze.4), kind=kOutput, calls=%fused_computation | convolution fusion | flops 20734851072 | bytes 17897216 | tf_op jit(solution)/shard_map/dot_general | solution.py:23
  181.9 0.4 slice_subtract_fusion
  182.3 0.7 fusion.25
  183.0 0.4 fusion.21
  183.4 2.1 pad_maximum_fusion
  185.5 5.6 %copy.29 = f32[416,3,721]{0,2,1:T(8,128)} copy(f32[416,3,721]{2,0,1:T(8,128)} %pad_maximum_fusion) | data formatting | bytes 7198464 | tf_op jit(solution)/shard_map/stack | solution.py:41
  191.1 4.9 %reshape.126 = f32[416,2163]{0,1:T(8,128)} reshape(f32[416,3,721]{0,2,1:T(8,128)} %copy.29) | data formatting | bytes 7198464 | tf_op jit(solution)/shard_map/reshape | solution.py:93
  196.0 5.2 %fusion.7 = f32[15,2163]{1,0:T(8,128)} fusion(f32[416,2163]{0,1:T(8,128)} %reshape.126, f32[416]{0:T(512)S(1)} %fusion.37, s32[416]{0:T(512)S(1)} %fusion.29), kind=kOutput, calls=%fused_computation.8 | convolution fusion | flops 162871488 | bytes 3732340 | tf_op jit(solution)/shard_map/dot_general | solution.py:100
  201.2 54.4 %all-reduce.2.cloned.1.call-done = f32[15,2163]{1,0:T(8,128)} async-done(((f32[15,2163]{1,0:T(8,128)}), f32[15,2163]{1,0:T(8,128)}) %all-reduce.2.cloned.1.call-update) | async-done | bytes 129796 | tf_op jit(solution)/shard_map/psum | solution.py:103
  255.6 11.1 %all-gather = f32[4,15,2163]{2,1,0:T(8,128)S(1)} all-gather(f32[1,15,2163]{2,1,0:T(8,128)} %bitcast.43), channel_id=1, replica_groups=mesh['lat'=8,'lon'=4] {'lon'}, dimensions={0}, use_global_device_ids=true | all-gather | bytes 648900 | tf_op jit(solution)/shard_map/all_gather | solution.py:104
  266.8 0.4 fusion.26
  267.2 0.4 reshape.127
  267.7 0.9 copy.30
  (23 shorter events, 0.8 us)
Async XLA Ops:
  14.8 4.8 %copy-start = (f32[360,1664]{1,0:T(8,128)S(1)}, f32[360,1664]{1,0:T(8,128)}, u32[]{:S(2)}) copy-start(f32[360,1664]{1,0:T(8,128)} %param.3) | copy-start | bytes 7188484
  14.8 34.9 %all-to-all-start.1 = ((f32[360,4,416]{0,2,1:T(8,128)}), f32[360,4,416]{0,2,1:T(8,128)}, u32[]{:S(2)}, u32[]{:S(2)}) async-start(f32[360,4,416]{0,2,1:T(8,128)} %bitcast.41), calls=%async_computation.1 | async-start | bytes 5111808 | tf_op jit(solution)/shard_map/all_to_all | solution.py:83
  49.7 95.4 %all-to-all-start = ((f32[360,4,416]{0,2,1:T(8,128)}), f32[360,4,416]{0,2,1:T(8,128)S(1)}, u32[]{:S(2)}, u32[]{:S(2)}) async-start(f32[360,4,416]{0,2,1:T(8,128)} %bitcast.39), calls=%async_computation | async-start | bytes 5111808 | tf_op jit(solution)/shard_map/all_to_all | solution.py:82
  53.3 202.3 %all-reduce.2.cloned.1.call-start = ((), (), s32[]{:S(2)}) async-start(), calls=%async_computation.2 | async-start | bytes 278528 | tf_op jit(solution)/shard_map/psum | solution.py:103
  148.2 4.2 %copy-start.1 = (f32[1440,416]{0,1:T(8,128)S(1)}, f32[1440,416]{0,1:T(8,128)}, u32[]{:S(2)}) copy-start(f32[1440,416]{0,1:T(8,128)} %squeeze.5) | copy-start | bytes 7188484
Sparse Core Ops, SparseCore 0:
  201.3 54.3 all-reduce.1
where the time goes:
time: 276 us; the launch traced here: 275 us
  waiting for transfers between devices  77.7 us (28%)
  blocking collectives  66.9 us (24%)
  local copies, waits for them, and re-layouts  42.9 us (16%)
  matrix products  35 us (13%)
  other arithmetic  29 us (11%)
  between operations  15.5 us (6%)
  starting transfers between devices  8.44 us (3%)
    psum x1, blocking collectives, local(): lax.psum(skill_terms, ('lat', 'lon')) / (lon_total * weight_total)  55.8 us
    psum x1, waiting for transfers between devices, local(): band_sum = lax.psum(band_sum, 'lat')  54.4 us
    dot_general x1, matrix products, transform_columns(): lax.dot_general(stacked, table, (((0,), (0,)), ((), ())), precision=lax.P...  29.4 us
    all_to_all x1, waiting for transfers between devices, local(): lax.all_to_all(true_blocks, 'lon', split_axis=1, concat_axis=0, tiled=True)  23.2 us
    neg x1, other arithmetic, dft_table(): return jnp.concatenate([jnp.cos(angle), -jnp.sin(angle)], axis=1)  19.7 us
    all_gather x1, blocking collectives, local(): gathered = lax.all_gather(band_sum, 'lon', axis=0, tiled=True)  11.1 us
    unnamed x8, local copies, waits for them, and re-layouts  6.34 us
    another operation x1, local copies, waits for them, and re-layouts, row_powers(): jnp.stack([square(fore_coeffs), square(true_coeffs), square(diff_coeffs)]...  5.61 us
  transfers between devices with their start and end apart: 3, of which 2 were waited for; matrix products, arithmetic and copies ran while one was open for 15% of the time, Pallas kernels for 0%

commit v1 on v0

--- a/solution.py
+++ b/solution.py
@@ -109,7 +109,7 @@
         placer, gathered, precision=lax.Precision.HIGHEST, preferred_element_type=jnp.float32
     )
     energy_curves = summed.reshape(quantity_labels, 3, wave_count).transpose(1, 0, 2)
-    skill_means = lax.psum(skill_terms, ("lat", "lon")) / (lon_total * weight_total)
+    skill_means = lax.psum(lax.psum(skill_terms, "lat"), "lon") / (lon_total * weight_total)
     rms_error = jnp.sqrt(skill_means[0])
     anomaly_corr = skill_means[1] / jnp.sqrt(
         (skill_means[2] + epsilon) * (skill_means[3] + epsilon)

time: 276 us -> 246 us (0.89)
  blocking collectives: 66.9 us -> 36.7 us
    psum x1 -> x2, blocking collectives: 55.8 us -> 25.6 us  [the longest x1 13.4 us: local(): lax.psum(lax.psum(skill_terms, 'lat'), 'lon') / (lon_total * weight_total)]
  transfers between devices with their start and end apart: 3 -> 3, of which waited for: 2 -> 2; matrix products, arithmetic and copies ran while one was open for 15% -> 17% of each run, Pallas kernels for 0% -> 0%
where the time goes in v1:
time: 246 us; the launch traced here: 245 us
  waiting for transfers between devices  77.9 us (32%)
  local copies, waits for them, and re-layouts  42.9 us (17%)
  blocking collectives  36.7 us (15%)
  matrix products  35 us (14%)
  other arithmetic  29 us (12%)
  between operations  15.5 us (6%)
  starting transfers between devices  8.44 us (3%)
    psum x1, waiting for transfers between devices, local(): band_sum = lax.psum(band_sum, 'lat')  54.7 us
    dot_general x1, matrix products, transform_columns(): lax.dot_general(stacked, table, (((0,), (0,)), ((), ())), precision=lax.P...  29.4 us
    all_to_all x1, waiting for transfers between devices, local(): lax.all_to_all(true_blocks, 'lon', split_axis=1, concat_axis=0, tiled=True)  23.2 us
    neg x1, other arithmetic, dft_table(): return jnp.concatenate([jnp.cos(angle), -jnp.sin(angle)], axis=1)  19.7 us
    psum x1, blocking collectives, local(): lax.psum(lax.psum(skill_terms, 'lat'), 'lon') / (lon_total * weight_total)  13.4 us
    psum x1, blocking collectives, local(): lax.psum(skill_terms, 'lat')  12.2 us
    all_gather x1, blocking collectives, local(): gathered = lax.all_gather(band_sum, 'lon', axis=0, tiled=True)  11.1 us
    unnamed x8, local copies, waits for them, and re-layouts  6.34 us
  transfers between devices with their start and end apart: 3, of which 2 were waited for; matrix products, arithmetic and copies ran while one was open for 17% of the time, Pallas kernels for 0%

profile of v1, /device:TPU:8, one launch (start us, length us, event | category | flops | bytes accessed | tf_op | source)
XLA Modules:
  0.0 245.4 jit_solution(3181763924175955648)
XLA Ops:
  7.2 3.2 %copy.26 = f32[360,1664]{0,1:T(8,128)} copy(f32[360,1664]{1,0:T(8,128)} %param.4) | data formatting | bytes 4792320 | tf_op args[1]
  10.4 2.4 reshape.125
  12.8 1.9 copy.27
  14.8 4.8 %all-to-all-start.1 = ((f32[360,4,416]{0,2,1:T(8,128)}), f32[360,4,416]{0,2,1:T(8,128)}, u32[]{:S(2)}, u32[]{:S(2)}) async-start(f32[360,4,416]{0,2,1:T(8,128)} %bitcast.41), calls=%async_computation.1 | async-start | bytes 5111808 | tf_op jit(solution)/shard_map/all_to_all | solution.py:83
  19.6 2.2 copy.23
  21.7 2.4 reshape.124
  24.2 2.1 copy.24
  26.5 23.2 %all-to-all-done.1 = f32[360,4,416]{0,2,1:T(8,128)} async-done(((f32[360,4,416]{0,2,1:T(8,128)}), f32[360,4,416]{0,2,1:T(8,128)}, u32[]{:S(2)}, u32[]{:S(2)}) %all-to-all-start.1) | async-done | bytes 2396192 | tf_op jit(solution)/shard_map/all_to_all | solution.py:83
  49.7 3.6 %all-to-all-start = ((f32[360,4,416]{0,2,1:T(8,128)}), f32[360,4,416]{0,2,1:T(8,128)S(1)}, u32[]{:S(2)}, u32[]{:S(2)}) async-start(f32[360,4,416]{0,2,1:T(8,128)} %bitcast.39), calls=%async_computation | async-start | bytes 5111808 | tf_op jit(solution)/shard_map/all_to_all | solution.py:82
  53.4 4.3 %fusion.17 = (f32[1664]{0:T(1024)S(1)}, f32[1664]{0:T(1024)S(1)}, f32[1664]{0:T(1024)S(1)}, f32[1664]{0:T(1024)S(1)}) fusion(f32[360,1664]{1,0:T(8,128)} %param.3, f32[360,1664]{1,0:T(8,128)} %param.4, f32[1664]{0:T(1024)S(1)} %mul.171, f32[360,1664]{1,0:T(8,128)} %param.5), kind=kLoop, calls=%fused_computation.26 | loop fusion | flops 8379904 | bytes 7221760 | tf_op jit(solution)/shard_map/reduce_sum | solution.py:69
  58.1 0.7 cosine_reduce_fusion
  60.1 12.2 %psum.22 = f32[4,52]{1,0:T(4,128)S(1)} all-reduce(f32[4,52]{1,0:T(4,128)S(1)} %pad_maximum_fusion.1), channel_id=1, replica_groups=mesh['lat'=8,'lon'=4] {'lat'}, use_global_device_ids=true, to_apply=%region_10.11 | all-reduce | flops 208 | bytes 1664 | tf_op jit(solution)/shard_map/psum | solution.py:112
  72.4 13.4 %psum.23 = f32[4,52]{1,0:T(4,128)S(1)} all-reduce(f32[4,52]{1,0:T(4,128)S(1)} %psum.22), channel_id=1, replica_groups=mesh['lat'=8,'lon'=4] {'lon'}, use_global_device_ids=true, to_apply=%region_11.12 | all-reduce | flops 208 | bytes 1664 | tf_op jit(solution)/shard_map/psum | solution.py:112
  85.8 0.5 multiply_bitcast_fusion
  86.4 19.7 %sine_negate_fusion = (f32[1440,721]{1,0:T(8,128)}, f32[1440,721]{1,0:T(8,128)}) fusion(), kind=kLoop, calls=%fused_computation.12 | loop fusion | flops 10382400 | bytes 8305920 | tf_op jit(solution)/shard_map/neg | solution.py:19
  106.0 4.8 %copy.28 = f32[4,360,1,416]{1,0,3,2:T(4,128)} copy(f32[4,360,1,416]{1,3,0,2:T(8,128)} %bitcast.7) | data formatting | bytes 4792320 | tf_op jit(solution)/shard_map/all_to_all | solution.py:83
  110.9 4.0 %squeeze.5 = f32[1440,416]{0,1:T(8,128)} reshape(f32[4,360,1,416]{1,0,3,2:T(4,128)} %copy.28) | data formatting | bytes 4792320 | tf_op jit(solution)/shard_map/squeeze | solution.py:83
  114.9 3.1 %copy.25 = f32[4,360,1,416]{1,0,3,2:T(4,128)} copy(f32[4,360,1,416]{1,3,0,2:T(8,128)S(1)} %bitcast.40) | data formatting | bytes 4792320 | tf_op jit(solution)/shard_map/all_to_all | solution.py:82
  118.0 4.2 %squeeze.4 = f32[1440,416]{0,1:T(8,128)} reshape(f32[4,360,1,416]{1,0,3,2:T(4,128)} %copy.25) | data formatting | bytes 4792320 | tf_op jit(solution)/shard_map/squeeze | solution.py:82
  122.2 29.4 %fusion = f32[832,1442]{1,0:T(8,128)S(1)} fusion(f32[1440,721]{1,0:T(8,128)} %get-tuple-element.20, f32[1440,721]{1,0:T(8,128)} %get-tuple-element.21, f32[1440,416]{0,1:T(8,128)S(1)} %copy-done.1, f32[1440,416]{0,1:T(8,128)} %squeeze.4), kind=kOutput, calls=%fused_computation | convolution fusion | flops 20734851072 | bytes 17897216 | tf_op jit(solution)/shard_map/dot_general | solution.py:23
  151.7 0.4 slice_subtract_fusion
  152.1 0.7 fusion.25
  152.8 0.4 fusion.21
  153.2 2.1 pad_maximum_fusion
  155.3 5.6 %copy.29 = f32[416,3,721]{0,2,1:T(8,128)} copy(f32[416,3,721]{2,0,1:T(8,128)} %pad_maximum_fusion) | data formatting | bytes 7198464 | tf_op jit(solution)/shard_map/stack | solution.py:41
  160.9 4.9 %reshape.126 = f32[416,2163]{0,1:T(8,128)} reshape(f32[416,3,721]{0,2,1:T(8,128)} %copy.29) | data formatting | bytes 7198464 | tf_op jit(solution)/shard_map/reshape | solution.py:93
  165.8 5.2 %fusion.7 = f32[15,2163]{1,0:T(8,128)} fusion(f32[416,2163]{0,1:T(8,128)} %reshape.126, f32[416]{0:T(512)S(1)} %fusion.37, s32[416]{0:T(512)S(1)} %fusion.29), kind=kOutput, calls=%fused_computation.8 | convolution fusion | flops 162871488 | bytes 3732340 | tf_op jit(solution)/shard_map/dot_general | solution.py:100
  171.0 54.7 %all-reduce.2.cloned.1.call-done = f32[15,2163]{1,0:T(8,128)} async-done(((f32[15,2163]{1,0:T(8,128)}), f32[15,2163]{1,0:T(8,128)}) %all-reduce.2.cloned.1.call-update) | async-done | bytes 129796 | tf_op jit(solution)/shard_map/psum | solution.py:103
  225.7 11.1 %all-gather = f32[4,15,2163]{2,1,0:T(8,128)S(1)} all-gather(f32[1,15,2163]{2,1,0:T(8,128)} %bitcast.43), channel_id=1, replica_groups=mesh['lat'=8,'lon'=4] {'lon'}, dimensions={0}, use_global_device_ids=true | all-gather | bytes 648900 | tf_op jit(solution)/shard_map/all_gather | solution.py:104
  236.8 0.4 fusion.26
  237.3 0.4 reshape.127
  237.7 0.9 copy.30
  (24 shorter events, 1.0 us)
Async XLA Ops:
  14.8 4.8 %copy-start = (f32[360,1664]{1,0:T(8,128)S(1)}, f32[360,1664]{1,0:T(8,128)}, u32[]{:S(2)}) copy-start(f32[360,1664]{1,0:T(8,128)} %param.3) | copy-start | bytes 7188484
  14.8 34.9 %all-to-all-start.1 = ((f32[360,4,416]{0,2,1:T(8,128)}), f32[360,4,416]{0,2,1:T(8,128)}, u32[]{:S(2)}, u32[]{:S(2)}) async-start(f32[360,4,416]{0,2,1:T(8,128)} %bitcast.41), calls=%async_computation.1 | async-start | bytes 5111808 | tf_op jit(solution)/shard_map/all_to_all | solution.py:83
  49.7 65.3 %all-to-all-start = ((f32[360,4,416]{0,2,1:T(8,128)}), f32[360,4,416]{0,2,1:T(8,128)S(1)}, u32[]{:S(2)}, u32[]{:S(2)}) async-start(f32[360,4,416]{0,2,1:T(8,128)} %bitcast.39), calls=%async_computation | async-start | bytes 5111808 | tf_op jit(solution)/shard_map/all_to_all | solution.py:82
  53.3 172.4 %all-reduce.2.cloned.1.call-start = ((), (), s32[]{:S(2)}) async-start(), calls=%async_computation.2 | async-start | bytes 278528 | tf_op jit(solution)/shard_map/psum | solution.py:103
  118.0 4.2 %copy-start.1 = (f32[1440,416]{0,1:T(8,128)S(1)}, f32[1440,416]{0,1:T(8,128)}, u32[]{:S(2)}) copy-start(f32[1440,416]{0,1:T(8,128)} %squeeze.5) | copy-start | bytes 7188484
Sparse Core Ops, SparseCore 0:
  171.1 54.5 all-reduce.1
